TPU v7x, 256 devices: a whole 4x4x8 slice. The times are simulated.
256 devices in a mesh: section: 4 (over y_lo, core), dp: 8 (over z), mp: 8 (over y_hi, x).
Axes of the slice: x: 4, y: 4 (y_hi: 2, y_lo: 2; y = y_hi * 2 + y_lo), z: 8, core: 2. Of those that a mesh axis runs over, the one named last changes fastest.
Arguments:
- encoder_rows: bfloat16 [96, 256, 4096], P(('section', 'dp')), may hold values from -6 to 6
- w_key: bfloat16 [4096, 4096], P(('section', 'dp'), 'mp'), may hold values from -0.09375 to 0.09375
- w_value: bfloat16 [4096, 4096], P(('section', 'dp'), 'mp'), may hold values from -0.09375 to 0.09375
- query: bfloat16 [128, 128, 4096], P(('section', 'dp'), None, 'mp'), may hold values from -80 to 80
- grad_context: bfloat16 [128, 128, 4096], P(('section', 'dp'), None, 'mp'), may hold values from -6 to 6
- source: int32 [128], replicated, may hold values from 0 to 95, as said below
Outputs:
- context: bfloat16 [128, 128, 4096], P(('section', 'dp'), None, 'mp')
- grad_query: bfloat16 [128, 128, 4096], P(('section', 'dp'), None, 'mp')
- grad_kv_weights: float32 [2, 4096, 4096], P(None, ('section', 'dp'), 'mp')
Inputs may be any that keep to these rules, and one draw needn't show every extreme that they name: `source`: the sequences of one section index (the 32 consecutive sequences held at that section index) read only examples held at the same section index; the 4 sequences of one device read examples held at 4 different dp indices.
All inputs are finite; a program needn't handle non-finite values.
Results may differ from a plain program's by a relative error of at most 0.025.
The roundings to bfloat16 on the way count: a program that leaves them out, or rounds other values in their place, can miss the bound.
Values may be sent and summed in bfloat16 or wider, within the bound.
A program may use at most 128 MiB of HBM per device.

v0:
```python
import jax
import jax.numpy as jnp
from jax import lax
from jax.sharding import PartitionSpec as P

HEAD_DIM = 64


def per_device(encoder_rows, w_key, w_value, query, grad_context, source):
    ex_dev, seq_len, width = encoder_rows.shape
    dec_dev, q_rows, inner_dev = query.shape
    heads_dev = inner_dev // HEAD_DIM
    n_dp = lax.axis_size("dp")
    section_idx = lax.axis_index("section")
    dp_idx = lax.axis_index("dp")
    flat = encoder_rows.reshape(ex_dev * seq_len, width)
    key_acc = jnp.dot(
        flat,
        lax.all_gather(w_key, ("section", "dp"), axis=0, tiled=True),
        preferred_element_type=jnp.float32,
    )
    value_acc = jnp.dot(
        flat,
        lax.all_gather(w_value, ("section", "dp"), axis=0, tiled=True),
        preferred_element_type=jnp.float32,
    )
    keys = key_acc.astype(jnp.bfloat16).reshape(ex_dev, seq_len, inner_dev)
    values = value_acc.astype(jnp.bfloat16).reshape(ex_dev, seq_len, inner_dev)
    per_section = n_dp * dec_dev
    row_plan = lax.dynamic_slice_in_dim(source, section_idx * per_section, per_section).reshape(
        n_dp, dec_dev
    )
    holder_dp = row_plan // ex_dev - section_idx * n_dp
    local_ex = row_plan % ex_dev
    mine = holder_dp == dp_idx
    wanted = mine[:, :, None] & (
        local_ex[:, :, None] == jnp.arange(ex_dev, dtype=jnp.int32)[None, None, :]
    )
    pick = jnp.sum(wanted.astype(jnp.float32), axis=1).astype(jnp.bfloat16)
    my_holder = lax.dynamic_index_in_dim(holder_dp, dp_idx, 0, keepdims=False)
    send_keys = jnp.einsum("pk,ksc->psc", pick, keys, preferred_element_type=jnp.float32).astype(
        jnp.bfloat16
    )
    send_values = jnp.einsum(
        "pk,ksc->psc", pick, values, preferred_element_type=jnp.float32
    ).astype(jnp.bfloat16)
    recv_keys, recv_values = (
        lax.all_to_all(send_keys, "dp", split_axis=0, concat_axis=0, tiled=True),
        lax.all_to_all(send_values, "dp", split_axis=0, concat_axis=0, tiled=True),
    )
    tile_keys = jnp.take(recv_keys, my_holder, axis=0)
    tile_values = jnp.take(recv_values, my_holder, axis=0)
    q_four = query.reshape(dec_dev, q_rows, heads_dev, HEAD_DIM)
    g_four = grad_context.reshape(dec_dev, q_rows, heads_dev, HEAD_DIM)
    k_four = tile_keys.reshape(dec_dev, seq_len, heads_dev, HEAD_DIM)
    v_four = tile_values.reshape(dec_dev, seq_len, heads_dev, HEAD_DIM)
    scores = jnp.einsum("nthc,nuhc->nhtu", q_four, k_four, preferred_element_type=jnp.float32)
    top = jnp.max(scores, axis=-1, keepdims=True)
    expo = jnp.exp(scores - top)
    weights = expo / jnp.sum(expo, axis=-1, keepdims=True)
    probs = weights.astype(jnp.bfloat16)
    context = jnp.einsum(
        "nhtu,nuhc->nthc", probs, v_four, preferred_element_type=jnp.float32
    ).astype(jnp.bfloat16)
    dprobs = jnp.einsum("nthc,nuhc->nhtu", g_four, v_four, preferred_element_type=jnp.float32)
    delta = jnp.sum(weights * dprobs, axis=-1, keepdims=True)
    score_grads = (weights * (dprobs - delta)).astype(jnp.bfloat16)
    grad_query = jnp.einsum(
        "nhtu,nuhc->nthc", score_grads, k_four, preferred_element_type=jnp.float32
    ).astype(jnp.bfloat16)
    key_terms = jnp.einsum(
        "nhtu,nthc->nuhc", score_grads, q_four, preferred_element_type=jnp.float32
    ).astype(jnp.bfloat16)
    value_terms = jnp.einsum(
        "nhtu,nthc->nuhc", probs, g_four, preferred_element_type=jnp.float32
    ).astype(jnp.bfloat16)
    key_terms = key_terms.reshape(dec_dev, seq_len, inner_dev)
    value_terms = value_terms.reshape(dec_dev, seq_len, inner_dev)
    to_holder = (my_holder[:, None] == jnp.arange(n_dp, dtype=jnp.int32)[None, :]).astype(
        jnp.bfloat16
    )
    back_keys = jnp.einsum(
        "np,nsc->psc", to_holder, key_terms, preferred_element_type=jnp.float32
    ).astype(jnp.bfloat16)
    back_values = jnp.einsum(
        "np,nsc->psc", to_holder, value_terms, preferred_element_type=jnp.float32
    ).astype(jnp.bfloat16)
    ret_keys, ret_values = (
        lax.all_to_all(back_keys, "dp", split_axis=0, concat_axis=0, tiled=True),
        lax.all_to_all(back_values, "dp", split_axis=0, concat_axis=0, tiled=True),
    )
    summed_keys = jnp.einsum("pk,psc->ksc", pick, ret_keys, preferred_element_type=jnp.float32)
    summed_values = jnp.einsum("pk,psc->ksc", pick, ret_values, preferred_element_type=jnp.float32)
    grad_keys = summed_keys.astype(jnp.bfloat16).reshape(ex_dev * seq_len, inner_dev)
    grad_values = summed_values.astype(jnp.bfloat16).reshape(ex_dev * seq_len, inner_dev)
    part_keys = lax.dot_general(
        flat, grad_keys, (((0,), (0,)), ((), ())), preferred_element_type=jnp.float32
    )
    part_values = lax.dot_general(
        flat, grad_values, (((0,), (0,)), ((), ())), preferred_element_type=jnp.float32
    )
    grad_rows = lax.psum_scatter(
        jnp.concatenate([part_keys, part_values], axis=1).astype(jnp.bfloat16),
        ("section", "dp"),
        scatter_dimension=0,
        tiled=True,
    ).astype(jnp.float32)
    grad_kv_weights = jnp.stack([grad_rows[:, :inner_dev], grad_rows[:, inner_dev:]], axis=0)
    return (
        context.reshape(dec_dev, q_rows, inner_dev),
        grad_query.reshape(dec_dev, q_rows, inner_dev),
        grad_kv_weights,
    )


def solution(mesh):
    return jax.shard_map(
        per_device,
        mesh=mesh,
        in_specs=(
            P(("section", "dp"), None, None),
            P(("section", "dp"), "mp"),
            P(("section", "dp"), "mp"),
            P(("section", "dp"), None, "mp"),
            P(("section", "dp"), None, "mp"),
            P(),
        ),
        out_specs=(
            P(("section", "dp"), None, "mp"),
            P(("section", "dp"), None, "mp"),
            P(None, ("section", "dp"), "mp"),
        ),
        check_vma=False,
    )
```

profile of v0, /device:TPU:1, one launch (start us, length us, event | category | flops | bytes accessed | tf_op | source)
XLA Modules:
  0.0 623.1 jit_solution(6543163994647986004)
XLA Ops:
  10.6 102.7 %all-gather.3.cloned.1.call-done = bf16[4096,512]{1,0:T(8,128)(2,1)} async-done(((bf16[128,512]{1,0:T(8,128)(2,1)}), bf16[4096,512]{1,0:T(8,128)(2,1)}) %all-gather.3.cloned.1.call-update) | async-done | bytes 4194320 | tf_op jit(solution)/shard_map/all_gather | solution.py:24
  113.3 7.4 %convolution_convert_fusion.7 = bf16[768,512]{1,0:T(8,128)(2,1)S(1)} fusion(bf16[768,4096]{1,0:T(8,128)(2,1)} %bitcast.106, bf16[4096,512]{1,0:T(8,128)(2,1)} %all-gather.3.cloned.1.call-done), kind=kOutput, calls=%fused_computation.31 | convolution fusion | flops 3221618688 | bytes 11272192 | tf_op jit(solution)/shard_map/dot_general | solution.py:22
  121.8 2.0 copy.86
  123.9 10.4 %all-to-all-start = ((bf16[8,256,512]{2,1,0:T(8,128)(2,1)}), bf16[8,256,512]{2,1,0:T(8,128)(2,1)S(1)}, u32[]{:S(2)}, u32[]{:S(2)}) async-start(bf16[8,256,512]{2,1,0:T(8,128)(2,1)} %copy.86), calls=%async_computation | async-start | bytes 4194304 | tf_op jit(solution)/shard_map/all_to_all | solution.py:49
  134.2 108.1 %all-gather.5.cloned.1.call-done = bf16[4096,512]{1,0:T(8,128)(2,1)} async-done(((bf16[128,512]{1,0:T(8,128)(2,1)}), bf16[4096,512]{1,0:T(8,128)(2,1)}) %all-gather.5.cloned.1.call-update) | async-done | bytes 4194320 | tf_op jit(solution)/shard_map/all_gather | solution.py:19
  242.3 7.4 %convolution_convert_fusion.6 = bf16[768,512]{1,0:T(8,128)(2,1)S(1)} fusion(bf16[768,4096]{1,0:T(8,128)(2,1)} %bitcast.107, bf16[4096,512]{1,0:T(8,128)(2,1)} %all-gather.5.cloned.1.call-done), kind=kOutput, calls=%fused_computation.30 | convolution fusion | flops 3221618688 | bytes 11272192 | tf_op jit(solution)/shard_map/dot_general | solution.py:17
  252.8 10.6 %all-to-all-start.1 = ((bf16[8,256,512]{2,1,0:T(8,128)(2,1)}), bf16[8,256,512]{2,1,0:T(8,128)(2,1)}, u32[]{:S(2)}, u32[]{:S(2)}) async-start(bf16[8,256,512]{2,1,0:T(8,128)(2,1)} %copy.89), calls=%async_computation.1 | async-start | bytes 4194304 | tf_op jit(solution)/shard_map/all_to_all | solution.py:48
  266.8 48.4 %all-to-all-done.1 = bf16[8,256,512]{2,1,0:T(8,128)(2,1)} async-done(((bf16[8,256,512]{2,1,0:T(8,128)(2,1)}), bf16[8,256,512]{2,1,0:T(8,128)(2,1)}, u32[]{:S(2)}, u32[]{:S(2)}) %all-to-all-start.1) | async-done | bytes 2097184 | tf_op jit(solution)/shard_map/all_to_all | solution.py:48
  315.3 2.2 gather_fusion.1
  317.5 2.4 broadcast_select_fusion
  322.7 3.4 fusion.40
  326.1 3.3 fusion.3
  332.5 2.7 copy.96
  335.1 2.1 convolution_convert_fusion.1
  339.3 4.3 all-to-all-start.2
  343.6 4.1 convolution_convert_fusion.4
  347.8 2.6 copy.101
  350.4 2.1 convolution_convert_fusion
  352.6 2.0 copy.102
  354.6 37.2 %all-to-all-done.2 = bf16[8,256,512]{2,1,0:T(8,128)(2,1)} async-done(((bf16[8,256,512]{2,1,0:T(8,128)(2,1)}), bf16[8,256,512]{2,1,0:T(8,128)(2,1)}, u32[]{:S(2)}, u32[]{:S(2)}) %all-to-all-start.2) | async-done | bytes 2097184 | tf_op jit(solution)/shard_map/all_to_all | solution.py:89
  391.8 4.9 all-to-all-start.3
  397.0 3.0 fusion.14
  400.0 8.1 %fusion.1 = bf16[4096,512]{0,1:T(8,128)(2,1)} fusion(bf16[3,256,4096]{2,1,0:T(8,128)(2,1)} %param.8, bf16[3,256,512]{2,0,1:T(4,128)(2,1)S(1)} %fusion.14), kind=kOutput, calls=%fused_computation.6 | convolution fusion | flops 3223322624 | bytes 11272192 | tf_op jit(solution)/shard_map/dot_general | solution.py:96
  408.1 38.4 %all-to-all-done.3 = bf16[8,256,512]{2,1,0:T(8,128)(2,1)} async-done(((bf16[8,256,512]{2,1,0:T(8,128)(2,1)}), bf16[8,256,512]{2,1,0:T(8,128)(2,1)}, u32[]{:S(2)}, u32[]{:S(2)}) %all-to-all-start.3) | async-done | bytes 2097184 | tf_op jit(solution)/shard_map/all_to_all | solution.py:90
  446.4 3.0 fusion.17
  449.5 8.1 %fusion.2 = bf16[4096,512]{0,1:T(8,128)(2,1)} fusion(bf16[3,256,4096]{2,1,0:T(8,128)(2,1)} %param.8, bf16[3,256,512]{2,0,1:T(4,128)(2,1)S(1)} %fusion.17), kind=kOutput, calls=%fused_computation.7 | convolution fusion | flops 3223322624 | bytes 11272192 | tf_op jit(solution)/shard_map/dot_general | solution.py:99
  457.5 7.8 %pad_maximum_fusion = bf16[4096,1024]{0,1:T(8,128)(2,1)} fusion(bf16[4096,512]{0,1:T(8,128)(2,1)} %fusion.2, bf16[4096,512]{0,1:T(8,128)(2,1)} %fusion.1), kind=kLoop, calls=%fused_computation.3 | loop fusion | flops 16777216 | bytes 16777216 | tf_op jit(solution)/shard_map/concatenate | solution.py:103
  465.4 12.0 %copy.112 = bf16[4096,1024]{1,0:T(8,128)(2,1)} copy(bf16[4096,1024]{0,1:T(8,128)(2,1)} %pad_maximum_fusion) | data formatting | bytes 16777216
  477.4 3.8 convolution_convert_fusion.9
  481.2 2.0 copy.105
  484.5 2.0 copy.106
  486.5 127.8 %reduce-scatter.4.cloned.1.call-done = bf16[128,1024]{1,0:T(8,128)(2,1)} async-done(((bf16[4096,1024]{1,0:T(8,128)(2,1)}), bf16[128,1024]{1,0:T(8,128)(2,1)}) %reduce-scatter.4.cloned.1.call-update) | async-done | bytes 262160
  (49 shorter events, 22.6 us)
Async XLA Ops:
  7.2 106.2 %all-gather.3.cloned.1.call-start = ((), (), s32[]{:S(2)}) async-start(), calls=%async_computation.5 | async-start | bytes 4325376 | tf_op jit(solution)/shard_map/all_gather | solution.py:24
  7.9 234.4 %all-gather.5.cloned.1.call-start = ((), (), s32[]{:S(2)}) async-start(), calls=%async_computation.6 | async-start | bytes 4325376 | tf_op jit(solution)/shard_map/all_gather | solution.py:19
  123.9 128.9 %all-to-all-start = ((bf16[8,256,512]{2,1,0:T(8,128)(2,1)}), bf16[8,256,512]{2,1,0:T(8,128)(2,1)S(1)}, u32[]{:S(2)}, u32[]{:S(2)}) async-start(bf16[8,256,512]{2,1,0:T(8,128)(2,1)} %copy.86), calls=%async_computation | async-start | bytes 4194304 | tf_op jit(solution)/shard_map/all_to_all | solution.py:49
  250.8 12.6 %copy-start.4 = (bf16[4,128,512]{2,1,0:T(8,128)(2,1)S(1)}, bf16[4,128,512]{2,1,0:T(8,128)(2,1)}, u32[]{:S(2)}) copy-start(bf16[4,128,512]{2,1,0:T(8,128)(2,1)} %param.11) | copy-start | bytes 1572868
  252.8 62.5 %all-to-all-start.1 = ((bf16[8,256,512]{2,1,0:T(8,128)(2,1)}), bf16[8,256,512]{2,1,0:T(8,128)(2,1)}, u32[]{:S(2)}, u32[]{:S(2)}) async-start(bf16[8,256,512]{2,1,0:T(8,128)(2,1)} %copy.89), calls=%async_computation.1 | async-start | bytes 4194304 | tf_op jit(solution)/shard_map/all_to_all | solution.py:48
  263.7 59.1 %copy-start.1 = (bf16[4,128,512]{1,2,0:T(8,128)(2,1)}, bf16[4,128,512]{1,2,0:T(8,128)(2,1)S(1)}, u32[]{:S(2)}) copy-start(bf16[4,128,512]{1,2,0:T(8,128)(2,1)S(1)} %copy.91) | copy-start | bytes 1572868
  265.2 60.9 %copy-start.5 = (bf16[4,128,512]{1,2,0:T(8,128)(2,1)}, bf16[4,128,512]{1,2,0:T(8,128)(2,1)S(1)}, u32[]{:S(2)}) copy-start(bf16[4,128,512]{1,2,0:T(8,128)(2,1)S(1)} %copy.93) | copy-start | bytes 1572868
  322.7 3.4 copy-start.3
  326.1 3.5 copy-start
  329.5 1.1 copy-start.2
  339.3 52.5 %all-to-all-start.2 = ((bf16[8,256,512]{2,1,0:T(8,128)(2,1)}), bf16[8,256,512]{2,1,0:T(8,128)(2,1)}, u32[]{:S(2)}, u32[]{:S(2)}) async-start(bf16[8,256,512]{2,1,0:T(8,128)(2,1)} %copy.97), calls=%async_computation.2 | async-start | bytes 4194304 | tf_op jit(solution)/shard_map/all_to_all | solution.py:89
  391.8 54.6 %all-to-all-start.3 = ((bf16[8,256,512]{2,1,0:T(8,128)(2,1)}), bf16[8,256,512]{2,1,0:T(8,128)(2,1)}, u32[]{:S(2)}, u32[]{:S(2)}) async-start(bf16[8,256,512]{2,1,0:T(8,128)(2,1)} %copy.102), calls=%async_computation.3 | async-start | bytes 4194304 | tf_op jit(solution)/shard_map/all_to_all | solution.py:90
  396.7 217.6 %reduce-scatter.4.cloned.1.call-start = ((), (), s32[]{:S(2)}) async-start(), calls=%async_computation.7 | async-start | bytes 8650752
Sparse Core Ops, SparseCore 0:
  9.8 103.5 all-gather.2
  115.1 127.0 all-gather.4
  477.5 136.7 reduce-scatter.3
where the time goes:
time: 624 us; the launch traced here: 623 us
  waiting for transfers between devices  464 us (74%)
  matrix products  61.1 us (10%)
  local copies, waits for them, and re-layouts  40.5 us (6%)
  starting transfers between devices  30.5 us (5%)
  between operations  14 us (2%)
  other arithmetic  13 us (2%)
    unnamed x4, waiting for transfers between devices  129 us
    all_gather x1, waiting for transfers between devices, per_device(): lax.all_gather(w_key, ('section', 'dp'), axis=0, tiled=True)  108 us
    all_gather x1, waiting for transfers between devices, per_device(): lax.all_gather(w_value, ('section', 'dp'), axis=0, tiled=True)  103 us
    all_to_all x1, waiting for transfers between devices, per_device(): lax.all_to_all(send_keys, 'dp', split_axis=0, concat_axis=0, tiled=True)  48.4 us
    all_to_all x1, waiting for transfers between devices, per_device(): lax.all_to_all(back_values, 'dp', split_axis=0, concat_axis=0, tiled=True)  38.4 us
    all_to_all x1, waiting for transfers between devices, per_device(): lax.all_to_all(back_keys, 'dp', split_axis=0, concat_axis=0, tiled=True)  37.2 us
    unnamed x19, local copies, waits for them, and re-layouts  20.1 us
  transfers between devices with their start and end apart: 7, of which 6 were waited for; matrix products, arithmetic and copies ran while one was open for 9% of the time, Pallas kernels for 0%

commit v1 on v0

--- a/solution.py
+++ b/solution.py
@@ -4,6 +4,15 @@
 from jax.sharding import PartitionSpec as P
 
 HEAD_DIM = 64
+get_face = lambda view, in_dim: jnp.concatenate(
+    jax.lax.all_to_all(
+        jnp.stack([view for _ in range(jax.lax.axis_size(("section", "dp")))], axis=0),
+        ("section", "dp"),
+        0,
+        0,
+    ),
+    axis=in_dim,
+)
 
 
 def per_device(encoder_rows, w_key, w_value, query, grad_context, source):
@@ -19,11 +28,7 @@
         lax.all_gather(w_key, ("section", "dp"), axis=0, tiled=True),
         preferred_element_type=jnp.float32,
     )
-    value_acc = jnp.dot(
-        flat,
-        lax.all_gather(w_value, ("section", "dp"), axis=0, tiled=True),
-        preferred_element_type=jnp.float32,
-    )
+    value_acc = jnp.dot(flat, get_face(w_value, in_dim=0), preferred_element_type=jnp.float32)
     keys = key_acc.astype(jnp.bfloat16).reshape(ex_dev, seq_len, inner_dev)
     values = value_acc.astype(jnp.bfloat16).reshape(ex_dev, seq_len, inner_dev)
     per_section = n_dp * dec_dev

time: 624 us -> 604 us (0.968)
  waiting for transfers between devices: 464 us -> 436 us
    all_gather x1 -> x0, waiting for transfers between devices: 103 us -> none  [per_device(): lax.all_gather(w_value, ('section', 'dp'), axis=0, tiled=True)]
    all_to_all x1, waiting for transfers between devices: 0.01 us -> 44.6 us  [per_device(): lax.all_to_all(send_values, 'dp', split_axis=0, concat_axis=0, tiled=True)]
    all_gather x1, waiting for transfers between devices: 108 us -> 145 us  [per_device(): lax.all_gather(w_key, ('section', 'dp'), axis=0, tiled=True)]
    all_to_all x0 -> x1, starting transfers between devices: none -> 11.3 us  [jax.lax.all_to_all(jnp.stack([view for _ in range(jax.lax.axis_size(('sec...]
    all_to_all x1, waiting for transfers between devices: 48.4 us -> 41.1 us  [per_device(): lax.all_to_all(send_keys, 'dp', split_axis=0, concat_axis=0, tiled=True)]
    unnamed x4 -> x3, waiting for transfers between devices: 129 us -> 128 us
    unnamed x19 -> x21, local copies, waits for them, and re-layouts: 20.1 us -> 20.1 us
  transfers between devices with their start and end apart: 7 -> 7, of which waited for: 6 -> 6; matrix products, arithmetic and copies ran while one was open for 9% -> 10% of each run, Pallas kernels for 0% -> 0%
where the time goes in v1:
time: 604 us; the launch traced here: 603 us
  waiting for transfers between devices  436 us (72%)
  matrix products  61.1 us (10%)
  local copies, waits for them, and re-layouts  43.9 us (7%)
  starting transfers between devices  35.7 us (6%)
  between operations  14.3 us (2%)
  other arithmetic  11.7 us (2%)
    all_gather x1, waiting for transfers between devices, per_device(): lax.all_gather(w_key, ('section', 'dp'), axis=0, tiled=True)  145 us
    unnamed x3, waiting for transfers between devices  128 us
    all_to_all x1, waiting for transfers between devices, per_device(): lax.all_to_all(send_values, 'dp', split_axis=0, concat_axis=0, tiled=True)  44.6 us
    all_to_all x1, waiting for transfers between devices, per_device(): lax.all_to_all(send_keys, 'dp', split_axis=0, concat_axis=0, tiled=True)  41.1 us
    all_to_all x1, waiting for transfers between devices, per_device(): lax.all_to_all(back_keys, 'dp', split_axis=0, concat_axis=0, tiled=True)  40.9 us
    all_to_all x1, waiting for transfers between devices, per_device(): lax.all_to_all(back_values, 'dp', split_axis=0, concat_axis=0, tiled=True)  36.8 us
    unnamed x21, local copies, waits for them, and re-layouts  20.1 us
  transfers between devices with their start and end apart: 7, of which 6 were waited for; matrix products, arithmetic and copies ran while one was open for 10% of the time, Pallas kernels for 0%

profile of v1, /device:TPU:1, one launch (start us, length us, event | category | flops | bytes accessed | tf_op | source)
XLA Modules:
  0.0 602.8 jit_solution(6927890814870697730)
XLA Ops:
  7.9 3.3 stack.8
  11.2 11.3 %all-to-all-start = ((bf16[32,128,512]{2,1,0:T(8,128)(2,1)}), bf16[32,128,512]{2,1,0:T(8,128)(2,1)}, u32[]{:S(2)}, u32[]{:S(2)}) async-start(bf16[32,128,512]{2,1,0:T(8,128)(2,1)} %stack.8), calls=%async_computation | async-start | bytes 8388608 | tf_op jit(solution)/shard_map/all_to_all | solution.py:8
  23.2 144.6 %all-gather.2.cloned.1.call-done = bf16[4096,512]{1,0:T(8,128)(2,1)} async-done(((bf16[128,512]{1,0:T(8,128)(2,1)}), bf16[4096,512]{1,0:T(8,128)(2,1)}) %all-gather.2.cloned.1.call-update) | async-done | bytes 4194320 | tf_op jit(solution)/shard_map/all_gather | solution.py:28
  167.9 7.4 %convolution_convert_fusion.6 = bf16[768,512]{1,0:T(8,128)(2,1)S(1)} fusion(bf16[768,4096]{1,0:T(8,128)(2,1)} %bitcast.107, bf16[4096,512]{1,0:T(8,128)(2,1)} %all-gather.2.cloned.1.call-done), kind=kOutput, calls=%fused_computation.30 | convolution fusion | flops 3221618688 | bytes 11272192 | tf_op jit(solution)/shard_map/dot_general | solution.py:26
  176.4 2.1 copy.89
  178.4 10.2 %all-to-all-start.2 = ((bf16[8,256,512]{2,1,0:T(8,128)(2,1)}), bf16[8,256,512]{2,1,0:T(8,128)(2,1)S(1)}, u32[]{:S(2)}, u32[]{:S(2)}) async-start(bf16[8,256,512]{2,1,0:T(8,128)(2,1)} %copy.89), calls=%async_computation.2 | async-start | bytes 4194304 | tf_op jit(solution)/shard_map/all_to_all | solution.py:53
  188.6 7.4 %convolution_convert_fusion.7 = bf16[768,512]{1,0:T(8,128)(2,1)S(1)} fusion(bf16[768,4096]{1,0:T(8,128)(2,1)} %bitcast.108, bf16[4096,512]{1,0:T(8,128)(2,1)} %bitcast.3), kind=kOutput, calls=%fused_computation.31 | convolution fusion | flops 3221618688 | bytes 11272192 | tf_op jit(solution)/shard_map/dot_general | solution.py:31
  199.1 41.1 %all-to-all-done.2 = bf16[8,256,512]{2,1,0:T(8,128)(2,1)S(1)} async-done(((bf16[8,256,512]{2,1,0:T(8,128)(2,1)}), bf16[8,256,512]{2,1,0:T(8,128)(2,1)S(1)}, u32[]{:S(2)}, u32[]{:S(2)}) %all-to-all-start.2) | async-done | bytes 2097184 | tf_op jit(solution)/shard_map/all_to_all | solution.py:53
  240.3 4.5 all-to-all-start.1
  248.2 44.6 %all-to-all-done.1 = bf16[8,256,512]{2,1,0:T(8,128)(2,1)} async-done(((bf16[8,256,512]{2,1,0:T(8,128)(2,1)}), bf16[8,256,512]{2,1,0:T(8,128)(2,1)}, u32[]{:S(2)}, u32[]{:S(2)}) %all-to-all-start.1) | async-done | bytes 2097184 | tf_op jit(solution)/shard_map/all_to_all | solution.py:54
  292.8 2.2 gather_fusion
  295.0 2.4 broadcast_select_fusion
  300.3 3.4 fusion.40
  303.6 3.3 fusion.3
  310.1 2.7 copy.96
  312.7 2.1 convolution_convert_fusion.1
  316.9 5.1 all-to-all-start.3
  321.9 4.1 convolution_convert_fusion.4
  326.0 2.6 copy.101
  328.7 2.1 convolution_convert_fusion
  332.9 40.9 %all-to-all-done.3 = bf16[8,256,512]{2,1,0:T(8,128)(2,1)} async-done(((bf16[8,256,512]{2,1,0:T(8,128)(2,1)}), bf16[8,256,512]{2,1,0:T(8,128)(2,1)}, u32[]{:S(2)}, u32[]{:S(2)}) %all-to-all-start.3) | async-done | bytes 2097184 | tf_op jit(solution)/shard_map/all_to_all | solution.py:94
  373.7 4.3 all-to-all-start.4
  378.3 3.0 fusion.14
  381.4 8.1 %fusion.1 = bf16[4096,512]{0,1:T(8,128)(2,1)} fusion(bf16[3,256,4096]{2,1,0:T(8,128)(2,1)} %param.8, bf16[3,256,512]{2,0,1:T(4,128)(2,1)S(1)} %fusion.14), kind=kOutput, calls=%fused_computation.6 | convolution fusion | flops 3223322624 | bytes 11272192 | tf_op jit(solution)/shard_map/dot_general | solution.py:101
  389.4 36.8 %all-to-all-done.4 = bf16[8,256,512]{2,1,0:T(8,128)(2,1)} async-done(((bf16[8,256,512]{2,1,0:T(8,128)(2,1)}), bf16[8,256,512]{2,1,0:T(8,128)(2,1)}, u32[]{:S(2)}, u32[]{:S(2)}) %all-to-all-start.4) | async-done | bytes 2097184 | tf_op jit(solution)/shard_map/all_to_all | solution.py:95
  426.2 3.0 fusion.17
  429.2 8.1 %fusion.2 = bf16[4096,512]{0,1:T(8,128)(2,1)} fusion(bf16[3,256,4096]{2,1,0:T(8,128)(2,1)} %param.8, bf16[3,256,512]{2,0,1:T(4,128)(2,1)S(1)} %fusion.17), kind=kOutput, calls=%fused_computation.7 | convolution fusion | flops 3223322624 | bytes 11272192 | tf_op jit(solution)/shard_map/dot_general | solution.py:104
  437.3 7.8 %pad_maximum_fusion = bf16[4096,1024]{0,1:T(8,128)(2,1)} fusion(bf16[4096,512]{0,1:T(8,128)(2,1)} %fusion.2, bf16[4096,512]{0,1:T(8,128)(2,1)} %fusion.1), kind=kLoop, calls=%fused_computation.3 | loop fusion | flops 16777216 | bytes 16777216 | tf_op jit(solution)/shard_map/concatenate | solution.py:108
  445.1 12.0 %copy.112 = bf16[4096,1024]{1,0:T(8,128)(2,1)} copy(bf16[4096,1024]{0,1:T(8,128)(2,1)} %pad_maximum_fusion) | data formatting | bytes 16777216
  457.2 3.8 convolution_convert_fusion.9
  460.9 2.0 copy.105
  466.3 127.4 %reduce-scatter.4.cloned.1.call-done = bf16[128,1024]{1,0:T(8,128)(2,1)} async-done(((bf16[4096,1024]{1,0:T(8,128)(2,1)}), bf16[128,1024]{1,0:T(8,128)(2,1)}) %reduce-scatter.4.cloned.1.call-update) | async-done | bytes 262160
  (51 shorter events, 24.6 us)
Async XLA Ops:
  7.2 160.7 %all-gather.2.cloned.1.call-start = ((), (), s32[]{:S(2)}) async-start(), calls=%async_computation.6 | async-start | bytes 4325376 | tf_op jit(solution)/shard_map/all_gather | solution.py:28
  11.2 11.3 %copy-start.6 = (s32[128]{0:T(128)S(1)}, s32[128]{0:T(128)}, u32[]{:S(2)}) copy-start(s32[128]{0:T(128)} %param.13) | copy-start | bytes 1540
  11.2 167.2 %all-to-all-start = ((bf16[32,128,512]{2,1,0:T(8,128)(2,1)}), bf16[32,128,512]{2,1,0:T(8,128)(2,1)}, u32[]{:S(2)}, u32[]{:S(2)}) async-start(bf16[32,128,512]{2,1,0:T(8,128)(2,1)} %stack.8), calls=%async_computation | async-start | bytes 8388608 | tf_op jit(solution)/shard_map/all_to_all | solution.py:8
  178.4 61.9 %all-to-all-start.2 = ((bf16[8,256,512]{2,1,0:T(8,128)(2,1)}), bf16[8,256,512]{2,1,0:T(8,128)(2,1)S(1)}, u32[]{:S(2)}, u32[]{:S(2)}) async-start(bf16[8,256,512]{2,1,0:T(8,128)(2,1)} %copy.89), calls=%async_computation.2 | async-start | bytes 4194304 | tf_op jit(solution)/shard_map/all_to_all | solution.py:53
  197.1 47.7 %copy-start.4 = (bf16[4,128,512]{2,1,0:T(8,128)(2,1)S(1)}, bf16[4,128,512]{2,1,0:T(8,128)(2,1)}, u32[]{:S(2)}) copy-start(bf16[4,128,512]{2,1,0:T(8,128)(2,1)} %param.11) | copy-start | bytes 1572868
  240.3 52.6 %all-to-all-start.1 = ((bf16[8,256,512]{2,1,0:T(8,128)(2,1)}), bf16[8,256,512]{2,1,0:T(8,128)(2,1)}, u32[]{:S(2)}, u32[]{:S(2)}) async-start(bf16[8,256,512]{2,1,0:T(8,128)(2,1)} %copy.86), calls=%async_computation.1 | async-start | bytes 4194304 | tf_op jit(solution)/shard_map/all_to_all | solution.py:54
  245.1 55.2 %copy-start.1 = (bf16[4,128,512]{1,2,0:T(8,128)(2,1)}, bf16[4,128,512]{1,2,0:T(8,128)(2,1)S(1)}, u32[]{:S(2)}) copy-start(bf16[4,128,512]{1,2,0:T(8,128)(2,1)S(1)} %copy.91) | copy-start | bytes 1572868
  246.6 57.0 %copy-start.5 = (bf16[4,128,512]{1,2,0:T(8,128)(2,1)}, bf16[4,128,512]{1,2,0:T(8,128)(2,1)S(1)}, u32[]{:S(2)}) copy-start(bf16[4,128,512]{1,2,0:T(8,128)(2,1)S(1)} %copy.93) | copy-start | bytes 1572868
  300.3 3.4 copy-start.3
  303.6 3.5 copy-start
  307.1 1.1 copy-start.2
  316.9 56.9 %all-to-all-start.3 = ((bf16[8,256,512]{2,1,0:T(8,128)(2,1)}), bf16[8,256,512]{2,1,0:T(8,128)(2,1)}, u32[]{:S(2)}, u32[]{:S(2)}) async-start(bf16[8,256,512]{2,1,0:T(8,128)(2,1)} %copy.97), calls=%async_computation.3 | async-start | bytes 4194304 | tf_op jit(solution)/shard_map/all_to_all | solution.py:94
  373.7 52.5 %all-to-all-start.4 = ((bf16[8,256,512]{2,1,0:T(8,128)(2,1)}), bf16[8,256,512]{2,1,0:T(8,128)(2,1)}, u32[]{:S(2)}, u32[]{:S(2)}) async-start(bf16[8,256,512]{2,1,0:T(8,128)(2,1)} %copy.102), calls=%async_computation.4 | async-start | bytes 4194304 | tf_op jit(solution)/shard_map/all_to_all | solution.py:95
  378.1 215.7 %reduce-scatter.4.cloned.1.call-start = ((), (), s32[]{:S(2)}) async-start(), calls=%async_computation.7 | async-start | bytes 8650752
Sparse Core Ops, SparseCore 0:
  9.8 158.0 all-gather.1
  457.3 136.4 reduce-scatter.3
